TPU v7x, 32 devices: a whole 2x2x4 slice. The times are simulated.
32 devices in a mesh: level: 8 (over z, y), bal: 4 (over x, core).
Axes of the slice: x: 2, y: 2, z: 4, core: 2. Of those that a mesh axis runs over, the one named last changes fastest.
Arguments:
- patches: float32 [640, 5, 4096], P(('level', 'bal')), may hold values from -6 to 6
- patch_ids: int32 [640], P(('level', 'bal')), may hold values from 0 to 639, each once
- live: int32 [32], P(('level', 'bal')), may hold values from 4 to 12, as said below
- counts: int32 [2, 32], P(None, ('level', 'bal')), may hold values from 0 to 4, as said below
- parent_of: int32 [640], replicated, may hold values from 0 to 15
Outputs:
- new_patches: float32 [640, 5, 4096], P(('level', 'bal'))
- new_ids: int32 [640], P(('level', 'bal'))
- coarse: float32 [16, 5, 512], P('level')
Inputs may be any that keep to these rules, and one draw needn't show every extreme that they name: In every level group one device holds exactly 12 live patches. counts[r, d] never exceeds the live patches of device d at the start of round r; in every round and level group some device sends exactly 4.
All inputs are finite; a program needn't handle non-finite values.
Results may differ from a plain program's by a relative error of at most 0.0003.
Values sent between devices are 32-bit elements; how exact they have to be, the bound alone decides.
A program may use at most 64 MiB of HBM per device.

v0:
```python
import jax
import jax.numpy as jnp
from jax import lax
from jax.sharding import PartitionSpec as P

EDGE = 16
VARS = 5
SEND_MOST = 4
PAR_DEV = 2


def from_partner(array, axis, stride):
    return lax.ppermute(array, axis, [(i, i ^ 1 << stride) for i in range(lax.axis_size(axis))])


def restrict(fine_rows):
    leading = fine_rows.shape[:-1]
    half_edge = EDGE // 2
    blocks = fine_rows.reshape(leading + (half_edge, 2, half_edge, 2, half_edge, 2))
    return jnp.mean(blocks, axis=(-5, -3, -1)).reshape(
        leading + (half_edge * half_edge * half_edge,)
    )


def take_top(fine_rows, fine_ids, held_count, sent_count):
    capacity = fine_rows.shape[0]
    lane_index = jnp.arange(SEND_MOST, dtype=jnp.int32)
    pick_index = jnp.clip(held_count - sent_count + lane_index, 0, capacity - 1)
    is_valid = lane_index < sent_count
    return (
        jnp.where(is_valid[:, None, None], fine_rows[pick_index], 0.0),
        jnp.where(is_valid, fine_ids[pick_index], -1),
    )


def place_rows(fine_rows, fine_ids, kept_count, in_rows, in_ids):
    capacity = fine_rows.shape[0]
    slot_index = jnp.arange(capacity, dtype=jnp.int32)
    offset = slot_index - kept_count
    is_hit = (offset >= 0) & (offset < SEND_MOST)
    place_index = jnp.clip(offset, 0, SEND_MOST - 1)
    is_kept = slot_index < kept_count
    new_rows = jnp.where(
        is_kept[:, None, None],
        fine_rows,
        jnp.where(is_hit[:, None, None], in_rows[place_index], 0.0),
    )
    new_ids = jnp.where(is_kept, fine_ids, jnp.where(is_hit, in_ids[place_index], -1))
    return (new_rows, new_ids)


def pairwise_move(fine_rows, fine_ids, held_count, counts, rounds):
    for turn_index in range(rounds):
        sent_count = counts[turn_index, 0]
        out_rows, out_ids = take_top(fine_rows, fine_ids, held_count, sent_count)
        in_rows, in_marks = from_partner((out_rows, out_ids.astype(jnp.float32)), "bal", turn_index)
        in_ids = in_marks.astype(jnp.int32)
        kept_count = held_count - sent_count
        fine_rows, fine_ids = place_rows(fine_rows, fine_ids, kept_count, in_rows, in_ids)
        held_count = kept_count + jnp.sum((in_ids >= 0).astype(jnp.int32))
    return (fine_rows, fine_ids)


def parent_sums(fine_rows, fine_ids, parent_of):
    capacity = fine_rows.shape[0]
    reduced = restrict(fine_rows).reshape(capacity, -1)
    parent = jnp.where(fine_ids >= 0, parent_of[jnp.clip(fine_ids, 0, parent_of.shape[0] - 1)], -1)
    wanted = jnp.arange(lax.axis_size("level") * PAR_DEV, dtype=jnp.int32)
    one_hot = (wanted[:, None] == parent[None, :]).astype(jnp.float32)
    level_sums = lax.psum_scatter(
        jnp.dot(one_hot, reduced, precision=lax.Precision.HIGHEST),
        "level",
        scatter_dimension=0,
        tiled=True,
    )
    group_sums = lax.psum(level_sums, "bal")
    return group_sums.reshape(PAR_DEV, VARS, -1)


def per_device(patches, patch_ids, live, counts, parent_of):
    capacity = patches.shape[0]
    group = lax.axis_size("bal")
    rounds = group.bit_length() - 1
    slot_index = jnp.arange(capacity, dtype=jnp.int32)
    held_count = live[0]
    is_kept = slot_index < held_count
    fine_rows = jnp.where(is_kept[:, None, None], patches, 0.0)
    fine_ids = jnp.where(is_kept, patch_ids, -1)
    coarse = parent_sums(fine_rows, fine_ids, parent_of)
    fine_rows, fine_ids = pairwise_move(fine_rows, fine_ids, held_count, counts, rounds)
    return (fine_rows, fine_ids, coarse)


def solution(mesh):
    return jax.shard_map(
        per_device,
        mesh=mesh,
        in_specs=(
            P(("level", "bal"), None, None),
            P(("level", "bal")),
            P(("level", "bal")),
            P(None, ("level", "bal")),
            P(),
        ),
        out_specs=(P(("level", "bal"), None, None), P(("level", "bal")), P("level", None, None)),
        check_vma=False,
    )
```

profile of v0, /device:TPU:0, one launch (start us, length us, event | category | flops | bytes accessed | tf_op | source)
XLA Modules:
  0.0 143.0 jit_solution(11142344460428278387)
XLA Ops:
  7.2 0.0 copy-start
  7.2 0.0 all-reduce.3.cloned.1.call-start
  7.2 1.3 fusion.13
  9.2 0.6 iota_compare_fusion.5
  10.4 0.0 copy-start.1
  10.4 2.7 %copy_select_fusion = f32[20,5,4096]{2,1,0:T(8,128)S(1)} fusion(f32[20,5,4096]{2,0,1:T(8,128)} %param.5, pred[20]{0:T(512)(128)(4,1)S(1)} %iota_compare_fusion.4), kind=kLoop, calls=%fused_computation.7 | loop fusion | flops 409600 | bytes 3276820 | tf_op jit(solution)/shard_map/jit(_where)/select_n | solution.py:87
  13.1 0.6 gather_fusion.1
  13.7 0.9 broadcast_select_fusion.1
  14.6 0.5 collective-permute-start.1
  15.1 0.0 copy-done.1
  15.1 0.6 gather_fusion
  15.7 0.6 select_convert_fusion.1
  16.3 0.1 collective-permute-start
  16.4 6.2 %copy.14 = f32[20,5,4096]{0,2,1:T(8,128)} copy(f32[20,5,4096]{2,1,0:T(8,128)S(1)} %copy_select_fusion) | data formatting | bytes 3276800 | tf_op jit(solution)/shard_map/jit(_where)/select_n | solution.py:87
  22.6 0.6 iota_compare_fusion.2
  23.3 10.6 %reduce_sum.19 = f32[20,5,8,8,8]{0,4,3,2,1:T(8,128)S(1)} reduce(f32[20,5,8,2,8,2,8,2]{0,7,6,5,4,3,2,1:T(2,128)} %bitcast.30, f32[]{:T(128)} %constant.3.clone.1), dimensions={3,5,7}, to_apply=%region_1.2 | reduce | flops 358400 | bytes 1843204 | tf_op jit(solution)/shard_map/reduce_sum | solution.py:20
  33.9 0.0 copy-start.2
  33.9 0.2 broadcast_multiply_fusion
  34.1 0.0 copy-done
  34.1 0.7 gather_fusion.6
  34.7 0.0 copy-done.2
  34.7 0.6 dynamic-slice
  36.0 0.0 collective-permute-done
  36.0 0.6 fusion.6
  38.0 0.7 fusion.12
  38.7 2.5 %compare_select_fusion.11 = (s32[20]{0:T(128)S(1)}, s32[20]{0:T(128)S(1)}) fusion(s32[20]{0:T(128)S(1)} %gather_fusion.6, s32[20]{0:T(128)S(1)} %get-tuple-element.10, s32[]{:T(128)} %bitcast.10, s32[]{:T(128)} %bitcast.9, s32[]{:T(128)} %bitcast.8, s32[]{:T(128)} %bitcast.7, s32[]{:T(128)S(6)} %sub.42), kind=kLoop, calls=%fused_computation.32 | loop fusion | flops 400 | bytes 340 | tf_op jit(solution)/shard_map/jit(_where)/select_n | solution.py:67
  41.2 0.6 gather_fusion.5
  41.8 0.7 select_convert_fusion
  42.5 3.0 %collective-permute-start.3 = (f32[4]{0:T(128)S(1)}, f32[4]{0:T(128)S(1)}, u32[]{:S(2)}, u32[]{:S(2)}) collective-permute-start(f32[4]{0:T(128)S(1)} %select_convert_fusion), channel_id=1, source_target_pairs={{0,2},{1,3},{2,0},{3,1},{4,6},{5,7},{6,4},{7,5},{8,10},{9,11},{10,... | collective-permute-start | bytes 56 | tf_op jit(solution)/shard_map/ppermute | solution.py:13
  45.5 1.4 fusion
  46.9 0.0 all-reduce.3.cloned.1.call-update
  46.9 0.1 collective-permute-done.3
  47.0 0.7 fusion.11
  47.7 3.0 %fusion.5 = s32[20]{0:T(128)} fusion(s32[20]{0:T(128)S(1)} %get-tuple-element.12, s32[]{:T(128)} %bitcast.11, s32[]{:T(128)} %bitcast.12, s32[]{:T(128)} %bitcast.13, s32[]{:T(128)} %bitcast.14, s32[]{:T(128)S(6)} %sub.43), kind=kLoop, calls=%fused_computation.39 | loop fusion | flops 360 | bytes 180 | tf_op jit(solution)/shard_map/jit(_where)/select_n | solution.py:48
  50.7 0.0 collective-permute-done.1
  50.7 2.2 %gather_fusion.2 = f32[20,5,4096]{2,1,0:T(8,128)} fusion(f32[4,5,4096]{2,1,0:T(8,128)S(1)} %collective-permute-done.1, s32[1024]{0:T(1024)S(1)} %pad_clamp_fusion.3), kind=kCustom, calls=%fused_computation.2 | custom fusion | bytes 3276880 | tf_op jit(solution)/shard_map/gather | solution.py:46
  52.9 3.8 %select_select_fusion.1 = f32[20,5,4096]{2,1,0:T(8,128)S(1)} fusion(f32[20,5,4096]{2,1,0:T(8,128)} %gather_fusion.2, pred[20]{0:T(512)(128)(4,1)S(1)} %get-tuple-element.23, pred[20]{0:T(512)(128)(4,1)S(1)} %get-tuple-element.24, f32[20,5,4096]{2,0,1:T(8,128)} %param.5, pred[20]{0:T(512)(128)(4,1)S(1)} %iota_compare_fusion.4), kind=kLoop, calls=%fused_computation.9 | loop fusion | flops 1228800 | bytes 4915260 | tf_op jit(solution)/shard_map/jit(_where)/select_n | solution.py:43
  56.8 0.6 gather_fusion.3
  57.3 0.9 broadcast_select_fusion
  58.2 2.0 %collective-permute-start.2 = (f32[4,5,4096]{2,1,0:T(8,128)}, f32[4,5,4096]{2,1,0:T(8,128)S(1)}, u32[]{:S(2)}, u32[]{:S(2)}) collective-permute-start(f32[4,5,4096]{2,1,0:T(8,128)} %broadcast_select_fusion), channel_id=1, source_target_pairs={{0,2},{1,3},{2,0},{3,1},{4,6},{5,7},{6,4},{7,5},{8,10},{9,11},{10,... | collective-permute-start | bytes 983048 | tf_op jit(solution)/shard_map/ppermute | solution.py:13
  60.3 57.1 %all-reduce.3.cloned.1.call-done = f32[16,2560]{1,0:T(8,128)} async-done(((f32[16,2560]{1,0:T(8,128)}), f32[16,2560]{1,0:T(8,128)}) %all-reduce.3.cloned.1.call-update) | async-done | bytes 163856
  117.4 0.9 constant_dynamic-slice_fusion
  118.3 10.3 %psum.7 = f32[2,5,512]{2,1,0:T(8,128)S(1)} all-reduce(f32[2,5,512]{2,1,0:T(8,128)S(1)} %reshape.127), channel_id=1, replica_groups=mesh['level'=8,'bal'=4] {'bal'}, use_global_device_ids=true, to_apply=%region_3.4 | all-reduce | flops 5120 | bytes 40960 | tf_op jit(solution)/shard_map/psum | solution.py:76
  128.6 0.6 copy.16
  129.2 0.0 collective-permute-done.2
  129.2 2.2 %gather_fusion.4 = f32[20,5,4096]{2,1,0:T(8,128)} fusion(f32[4,5,4096]{2,1,0:T(8,128)S(1)} %collective-permute-done.2, s32[1024]{0:T(1024)S(1)} %pad_clamp_fusion.1), kind=kCustom, calls=%fused_computation.4 | custom fusion | bytes 3276880 | tf_op jit(solution)/shard_map/gather | solution.py:46
  131.5 2.4 %select_select_fusion = f32[20,5,4096]{2,1,0:T(8,128)S(1)} fusion(f32[20,5,4096]{2,1,0:T(8,128)S(1)} %select_select_fusion.1, f32[20,5,4096]{2,1,0:T(8,128)} %gather_fusion.4, pred[20]{0:T(512)(128)(4,1)S(1)} %get-tuple-element.25, pred[20]{0:T(512)(128)(4,1)S(1)} %get-tuple-element.26), kind=kLoop, calls=%fused_computation.8 | loop fusion | flops 819200 | bytes 4915240 | tf_op jit(solution)/shard_map/jit(_where)/select_n | solution.py:43
  133.9 2.2 %copy.15 = f32[20,5,4096]{2,0,1:T(8,128)} copy(f32[20,5,4096]{2,1,0:T(8,128)S(1)} %select_select_fusion) | data formatting | bytes 3276800
  (16 shorter events, 0.1 us)
Async XLA Ops:
  7.2 26.9 %copy-start = (s32[640]{0:T(1024)S(1)}, s32[640]{0:T(1024)}, u32[]{:S(2)}) copy-start(s32[640]{0:T(1024)} %param.9) | copy-start | bytes 7684
  7.2 110.2 %all-reduce.3.cloned.1.call-start = ((), (), s32[]{:S(2)}) async-start(), calls=%async_computation | async-start | bytes 327680
  10.4 4.7 %copy-start.1 = (s32[20]{0:T(128)S(1)}, s32[20]{0:T(128)}, u32[]{:S(2)}) copy-start(s32[20]{0:T(128)} %param.6) | copy-start | bytes 244
  14.6 36.1 %collective-permute-start.1 = (f32[4,5,4096]{2,1,0:T(8,128)}, f32[4,5,4096]{2,1,0:T(8,128)S(1)}, u32[]{:S(2)}, u32[]{:S(2)}) collective-permute-start(f32[4,5,4096]{2,1,0:T(8,128)} %broadcast_select_fusion.1), channel_id=1, source_target_pairs={{0,1},{1,0},{2,3},{3,2},{4,5},{5,4},{6,7},{7,6},{8,9},{9,8},{10,11... | collective-permute-start | bytes 983048 | tf_op jit(solution)/shard_map/ppermute | solution.py:13
  16.3 19.7 %collective-permute-start = (f32[4]{0:T(128)S(1)}, f32[4]{0:T(128)S(1)}, u32[]{:S(2)}, u32[]{:S(2)}) collective-permute-start(f32[4]{0:T(128)S(1)} %select_convert_fusion.1), channel_id=1, source_target_pairs={{0,1},{1,0},{2,3},{3,2},{4,5},{5,4},{6,7},{7,6},{8,9},{9,8},{10,11... | collective-permute-start | bytes 56 | tf_op jit(solution)/shard_map/ppermute | solution.py:13
  33.9 0.9 copy-start.2
  42.5 4.6 %collective-permute-start.3 = (f32[4]{0:T(128)S(1)}, f32[4]{0:T(128)S(1)}, u32[]{:S(2)}, u32[]{:S(2)}) collective-permute-start(f32[4]{0:T(128)S(1)} %select_convert_fusion), channel_id=1, source_target_pairs={{0,2},{1,3},{2,0},{3,1},{4,6},{5,7},{6,4},{7,5},{8,10},{9,11},{10,... | collective-permute-start | bytes 56 | tf_op jit(solution)/shard_map/ppermute | solution.py:13
  58.2 71.0 %collective-permute-start.2 = (f32[4,5,4096]{2,1,0:T(8,128)}, f32[4,5,4096]{2,1,0:T(8,128)S(1)}, u32[]{:S(2)}, u32[]{:S(2)}) collective-permute-start(f32[4,5,4096]{2,1,0:T(8,128)} %broadcast_select_fusion), channel_id=1, source_target_pairs={{0,2},{1,3},{2,0},{3,1},{4,6},{5,7},{6,4},{7,5},{8,10},{9,11},{10,... | collective-permute-start | bytes 983048 | tf_op jit(solution)/shard_map/ppermute | solution.py:13
Sparse Core Ops, SparseCore 0:
  47.0 70.3 all-reduce.2
where the time goes:
time: 144 us; the launch traced here: 143 us
  waiting for transfers between devices  57.3 us (40%)
  other arithmetic  30.1 us (21%)
  local copies, waits for them, and re-layouts  20.8 us (14%)
  between operations  17.4 us (12%)
  blocking collectives  10.3 us (7%)
  starting transfers between devices  5.65 us (4%)
    unnamed x2, waiting for transfers between devices  57.2 us
    reduce_sum x1, other arithmetic, restrict(): jnp.mean(blocks, axis=(-5, -3, -1))  10.6 us
    psum x1, blocking collectives, parent_sums(): group_sums = lax.psum(level_sums, 'bal')  10.3 us
    select_n x2, other arithmetic, place_rows(): jnp.where(is_kept[:, None, None], fine_rows, jnp.where(is_hit[:, None, No...  6.28 us
    select_n x1, local copies, waits for them, and re-layouts, per_device(): fine_rows = jnp.where(is_kept[:, None, None], patches, 0.0)  6.24 us
    ppermute x4, starting transfers between devices, from_partner(): lax.ppermute(array, axis, [(i, i ^ 1 << stride) for i in range(lax.axis_s...  5.62 us
    gather x2, local copies, waits for them, and re-layouts, place_rows(): in_rows[place_index]  4.45 us
    unnamed x10, local copies, waits for them, and re-layouts  4.34 us
  transfers between devices with their start and end apart: 5, of which 2 were waited for; matrix products, arithmetic and copies ran while one was open for 28% of the time, Pallas kernels for 0%

commit v1 on v0

--- a/solution.py
+++ b/solution.py
@@ -73,7 +73,8 @@
         scatter_dimension=0,
         tiled=True,
     )
-    group_sums = lax.psum(level_sums, "bal")
+    pieces = lax.all_gather(level_sums, "bal", axis=0, tiled=False)
+    group_sums = pieces.sum(axis=0)
     return group_sums.reshape(PAR_DEV, VARS, -1)
 
 

time: 144 us -> 139 us (0.965)
  blocking collectives: 10.3 us -> 5.28 us
    psum x1 -> x0, blocking collectives: 10.3 us -> none  [parent_sums(): group_sums = lax.psum(level_sums, 'bal')]
    all_gather x0 -> x1, blocking collectives: none -> 5.28 us  [parent_sums(): pieces = lax.all_gather(level_sums, 'bal', axis=0, tiled=False)]
    unnamed x10 -> x9, local copies, waits for them, and re-layouts: 4.34 us -> 3.72 us
  transfers between devices with their start and end apart: 5 -> 5, of which waited for: 2 -> 2; matrix products, arithmetic and copies ran while one was open for 28% -> 29% of each run, Pallas kernels for 0% -> 0%
where the time goes in v1:
time: 139 us; the launch traced here: 138 us
  waiting for transfers between devices  57.3 us (41%)
  other arithmetic  30.7 us (22%)
  local copies, waits for them, and re-layouts  20.2 us (15%)
  between operations  17.4 us (13%)
  starting transfers between devices  5.65 us (4%)
  blocking collectives  5.28 us (4%)
  matrix products  1.41 us (1%)
    unnamed x2, waiting for transfers between devices  57.2 us
    reduce_sum x1, other arithmetic, restrict(): jnp.mean(blocks, axis=(-5, -3, -1))  10.6 us
    select_n x2, other arithmetic, place_rows(): jnp.where(is_kept[:, None, None], fine_rows, jnp.where(is_hit[:, None, No...  6.28 us
    select_n x1, local copies, waits for them, and re-layouts, per_device(): fine_rows = jnp.where(is_kept[:, None, None], patches, 0.0)  6.24 us
    ppermute x4, starting transfers between devices, from_partner(): lax.ppermute(array, axis, [(i, i ^ 1 << stride) for i in range(lax.axis_s...  5.62 us
    all_gather x1, blocking collectives, parent_sums(): pieces = lax.all_gather(level_sums, 'bal', axis=0, tiled=False)  5.28 us
    gather x2, local copies, waits for them, and re-layouts, place_rows(): in_rows[place_index]  4.45 us
    unnamed x9, local copies, waits for them, and re-layouts  3.72 us
  transfers between devices with their start and end apart: 5, of which 2 were waited for; matrix products, arithmetic and copies ran while one was open for 29% of the time, Pallas kernels for 0%

profile of v1, /device:TPU:0, one launch (start us, length us, event | category | flops | bytes accessed | tf_op | source)
XLA Modules:
  0.0 138.0 jit_solution(9068475344349914477)
XLA Ops:
  7.2 0.0 copy-start
  7.2 0.0 all-reduce.3.cloned.1.call-start
  7.2 1.3 fusion.13
  9.2 0.6 iota_compare_fusion.5
  10.4 0.0 copy-start.1
  10.4 2.7 %copy_select_fusion = f32[20,5,4096]{2,1,0:T(8,128)S(1)} fusion(f32[20,5,4096]{2,0,1:T(8,128)} %param.5, pred[20]{0:T(512)(128)(4,1)S(1)} %iota_compare_fusion.4), kind=kLoop, calls=%fused_computation.7 | loop fusion | flops 409600 | bytes 3276820 | tf_op jit(solution)/shard_map/jit(_where)/select_n | solution.py:88
  13.1 0.6 gather_fusion.1
  13.7 0.9 broadcast_select_fusion.1
  14.6 0.5 collective-permute-start.1
  15.1 0.0 copy-done.1
  15.1 0.6 gather_fusion
  15.7 0.6 select_convert_fusion.1
  16.3 0.1 collective-permute-start
  16.4 6.2 %copy.12 = f32[20,5,4096]{0,2,1:T(8,128)} copy(f32[20,5,4096]{2,1,0:T(8,128)S(1)} %copy_select_fusion) | data formatting | bytes 3276800 | tf_op jit(solution)/shard_map/jit(_where)/select_n | solution.py:88
  22.6 0.6 iota_compare_fusion.2
  23.3 10.6 %reduce_sum.28 = f32[20,5,8,8,8]{0,4,3,2,1:T(8,128)S(1)} reduce(f32[20,5,8,2,8,2,8,2]{0,7,6,5,4,3,2,1:T(2,128)} %bitcast.33, f32[]{:T(128)} %constant.3.clone.1), dimensions={3,5,7}, to_apply=%region_1.2 | reduce | flops 358400 | bytes 1843204 | tf_op jit(solution)/shard_map/reduce_sum | solution.py:20
  33.9 0.0 copy-start.2
  33.9 0.2 broadcast_multiply_fusion
  34.1 0.0 copy-done
  34.1 0.7 gather_fusion.6
  34.7 0.0 copy-done.2
  34.7 0.6 dynamic-slice
  36.0 0.0 collective-permute-done
  36.0 0.6 fusion.6
  38.0 0.7 fusion.12
  38.7 2.5 %compare_select_fusion.11 = (s32[20]{0:T(128)S(1)}, s32[20]{0:T(128)S(1)}) fusion(s32[20]{0:T(128)S(1)} %gather_fusion.6, s32[20]{0:T(128)S(1)} %get-tuple-element.10, s32[]{:T(128)} %bitcast.10, s32[]{:T(128)} %bitcast.9, s32[]{:T(128)} %bitcast.8, s32[]{:T(128)} %bitcast.7, s32[]{:T(128)S(6)} %sub.42), kind=kLoop, calls=%fused_computation.33 | loop fusion | flops 400 | bytes 340 | tf_op jit(solution)/shard_map/jit(_where)/select_n | solution.py:67
  41.2 0.6 gather_fusion.5
  41.8 0.7 select_convert_fusion
  42.5 3.0 %collective-permute-start.3 = (f32[4]{0:T(128)S(1)}, f32[4]{0:T(128)S(1)}, u32[]{:S(2)}, u32[]{:S(2)}) collective-permute-start(f32[4]{0:T(128)S(1)} %select_convert_fusion), channel_id=1, source_target_pairs={{0,2},{1,3},{2,0},{3,1},{4,6},{5,7},{6,4},{7,5},{8,10},{9,11},{10,... | collective-permute-start | bytes 56 | tf_op jit(solution)/shard_map/ppermute | solution.py:13
  45.5 1.4 %fusion = f32[16,2560]{1,0:T(8,128)} fusion(f32[20,2560]{0,1:T(8,128)S(1)} %bitcast.34, s32[20]{0:T(128)S(1)} %get-tuple-element.11), kind=kOutput, calls=%fused_computation.15 | convolution fusion | flops 9830720 | bytes 368720 | tf_op jit(solution)/shard_map/dot_general | solution.py:71
  46.9 0.0 all-reduce.3.cloned.1.call-update
  46.9 0.1 collective-permute-done.3
  47.0 0.7 fusion.11
  47.7 3.0 %fusion.5 = s32[20]{0:T(128)} fusion(s32[20]{0:T(128)S(1)} %get-tuple-element.12, s32[]{:T(128)} %bitcast.11, s32[]{:T(128)} %bitcast.12, s32[]{:T(128)} %bitcast.13, s32[]{:T(128)} %bitcast.14, s32[]{:T(128)S(6)} %sub.43), kind=kLoop, calls=%fused_computation.40 | loop fusion | flops 360 | bytes 180 | tf_op jit(solution)/shard_map/jit(_where)/select_n | solution.py:48
  50.7 0.0 collective-permute-done.1
  50.7 2.2 %gather_fusion.2 = f32[20,5,4096]{2,1,0:T(8,128)} fusion(f32[4,5,4096]{2,1,0:T(8,128)S(1)} %collective-permute-done.1, s32[1024]{0:T(1024)S(1)} %pad_clamp_fusion.3), kind=kCustom, calls=%fused_computation.2 | custom fusion | bytes 3276880 | tf_op jit(solution)/shard_map/gather | solution.py:46
  52.9 3.8 %select_select_fusion.1 = f32[20,5,4096]{2,1,0:T(8,128)S(1)} fusion(f32[20,5,4096]{2,1,0:T(8,128)} %gather_fusion.2, pred[20]{0:T(512)(128)(4,1)S(1)} %get-tuple-element.23, pred[20]{0:T(512)(128)(4,1)S(1)} %get-tuple-element.24, f32[20,5,4096]{2,0,1:T(8,128)} %param.5, pred[20]{0:T(512)(128)(4,1)S(1)} %iota_compare_fusion.4), kind=kLoop, calls=%fused_computation.9 | loop fusion | flops 1228800 | bytes 4915260 | tf_op jit(solution)/shard_map/jit(_where)/select_n | solution.py:43
  56.8 0.6 gather_fusion.3
  57.3 0.9 broadcast_select_fusion
  58.2 2.0 %collective-permute-start.2 = (f32[4,5,4096]{2,1,0:T(8,128)}, f32[4,5,4096]{2,1,0:T(8,128)S(1)}, u32[]{:S(2)}, u32[]{:S(2)}) collective-permute-start(f32[4,5,4096]{2,1,0:T(8,128)} %broadcast_select_fusion), channel_id=1, source_target_pairs={{0,2},{1,3},{2,0},{3,1},{4,6},{5,7},{6,4},{7,5},{8,10},{9,11},{10,... | collective-permute-start | bytes 983048 | tf_op jit(solution)/shard_map/ppermute | solution.py:13
  60.3 57.1 %all-reduce.3.cloned.1.call-done = f32[16,2560]{1,0:T(8,128)} async-done(((f32[16,2560]{1,0:T(8,128)}), f32[16,2560]{1,0:T(8,128)}) %all-reduce.3.cloned.1.call-update) | async-done | bytes 163856
  117.4 0.9 dynamic-slice_bitcast_fusion
  118.3 5.3 %all-gather.1 = f32[4,2,2560]{2,1,0:T(2,128)S(1)} all-gather(f32[1,2,2560]{2,1,0:T(2,128)S(1)} %dynamic-slice_bitcast_fusion), channel_id=2, replica_groups=mesh['level'=8,'bal'=4] {'bal'}, dimensions={0}, use_global_device_ids=true | all-gather | bytes 102400 | tf_op jit(solution)/shard_map/all_gather | solution.py:76
  123.6 0.6 reduce_sum.29
  124.2 0.0 collective-permute-done.2
  124.2 2.2 %gather_fusion.4 = f32[20,5,4096]{2,1,0:T(8,128)} fusion(f32[4,5,4096]{2,1,0:T(8,128)S(1)} %collective-permute-done.2, s32[1024]{0:T(1024)S(1)} %pad_clamp_fusion.1), kind=kCustom, calls=%fused_computation.4 | custom fusion | bytes 3276880 | tf_op jit(solution)/shard_map/gather | solution.py:46
  126.5 2.4 %select_select_fusion = f32[20,5,4096]{2,1,0:T(8,128)S(1)} fusion(f32[20,5,4096]{2,1,0:T(8,128)S(1)} %select_select_fusion.1, f32[20,5,4096]{2,1,0:T(8,128)} %gather_fusion.4, pred[20]{0:T(512)(128)(4,1)S(1)} %get-tuple-element.25, pred[20]{0:T(512)(128)(4,1)S(1)} %get-tuple-element.26), kind=kLoop, calls=%fused_computation.8 | loop fusion | flops 819200 | bytes 4915240 | tf_op jit(solution)/shard_map/jit(_where)/select_n | solution.py:43
  128.9 2.2 %copy.13 = f32[20,5,4096]{2,0,1:T(8,128)} copy(f32[20,5,4096]{2,1,0:T(8,128)S(1)} %select_select_fusion) | data formatting | bytes 3276800
  (15 shorter events, 0.1 us)
Async XLA Ops:
  7.2 26.9 %copy-start = (s32[640]{0:T(1024)S(1)}, s32[640]{0:T(1024)}, u32[]{:S(2)}) copy-start(s32[640]{0:T(1024)} %param.9) | copy-start | bytes 7684
  7.2 110.2 %all-reduce.3.cloned.1.call-start = ((), (), s32[]{:S(2)}) async-start(), calls=%async_computation | async-start | bytes 327680
  10.4 4.7 %copy-start.1 = (s32[20]{0:T(128)S(1)}, s32[20]{0:T(128)}, u32[]{:S(2)}) copy-start(s32[20]{0:T(128)} %param.6) | copy-start | bytes 244
  14.6 36.1 %collective-permute-start.1 = (f32[4,5,4096]{2,1,0:T(8,128)}, f32[4,5,4096]{2,1,0:T(8,128)S(1)}, u32[]{:S(2)}, u32[]{:S(2)}) collective-permute-start(f32[4,5,4096]{2,1,0:T(8,128)} %broadcast_select_fusion.1), channel_id=1, source_target_pairs={{0,1},{1,0},{2,3},{3,2},{4,5},{5,4},{6,7},{7,6},{8,9},{9,8},{10,11... | collective-permute-start | bytes 983048 | tf_op jit(solution)/shard_map/ppermute | solution.py:13
  16.3 19.7 %collective-permute-start = (f32[4]{0:T(128)S(1)}, f32[4]{0:T(128)S(1)}, u32[]{:S(2)}, u32[]{:S(2)}) collective-permute-start(f32[4]{0:T(128)S(1)} %select_convert_fusion.1), channel_id=1, source_target_pairs={{0,1},{1,0},{2,3},{3,2},{4,5},{5,4},{6,7},{7,6},{8,9},{9,8},{10,11... | collective-permute-start | bytes 56 | tf_op jit(solution)/shard_map/ppermute | solution.py:13
  33.9 0.9 copy-start.2
  42.5 4.6 %collective-permute-start.3 = (f32[4]{0:T(128)S(1)}, f32[4]{0:T(128)S(1)}, u32[]{:S(2)}, u32[]{:S(2)}) collective-permute-start(f32[4]{0:T(128)S(1)} %select_convert_fusion), channel_id=1, source_target_pairs={{0,2},{1,3},{2,0},{3,1},{4,6},{5,7},{6,4},{7,5},{8,10},{9,11},{10,... | collective-permute-start | bytes 56 | tf_op jit(solution)/shard_map/ppermute | solution.py:13
  58.2 66.0 %collective-permute-start.2 = (f32[4,5,4096]{2,1,0:T(8,128)}, f32[4,5,4096]{2,1,0:T(8,128)S(1)}, u32[]{:S(2)}, u32[]{:S(2)}) collective-permute-start(f32[4,5,4096]{2,1,0:T(8,128)} %broadcast_select_fusion), channel_id=1, source_target_pairs={{0,2},{1,3},{2,0},{3,1},{4,6},{5,7},{6,4},{7,5},{8,10},{9,11},{10,... | collective-permute-start | bytes 983048 | tf_op jit(solution)/shard_map/ppermute | solution.py:13
Sparse Core Ops, SparseCore 0:
  47.0 70.3 all-reduce.2
